TPU v7x, 128 devices: a whole 4x4x4 slice. The times are simulated.
128 devices in a mesh: gx: 8 (over z, core), gy: 16 (over x, y).
Axes of the slice: x: 4, y: 4, z: 4, core: 2. Of those that a mesh axis runs over, the one named last changes fastest.
Arguments:
- tokens: bfloat16 [4096, 4096], P(('gx', 'gy')), may hold values from -3 to 3
- attn_gain: bfloat16 [4096], replicated, may hold values from 0.099609375 to 1.8984375
- mlp_gain: bfloat16 [4096], replicated, may hold values from 0.099609375 to 1.8984375
- w_query: bfloat16 [4096, 4096], P('gx', 'gy'), may hold values from -1 to 1
- w_key: bfloat16 [4096, 1024], P('gx', 'gy'), may hold values from -1 to 1
- value_projection: bfloat16 [4096, 1024], P('gx', 'gy'), may hold values from -0.09375 to 0.09375
- w_out: bfloat16 [4096, 4096], P('gy', 'gx'), may hold values from -0.09375 to 0.09375
- w_gate: bfloat16 [4096, 14336], P('gx', 'gy'), may hold values from -0.09375 to 0.09375
- w_up: bfloat16 [4096, 14336], P('gx', 'gy'), may hold values from -0.09375 to 0.09375
- w_down: bfloat16 [14336, 4096], P('gy', 'gx'), may hold values from -0.046875 to 0.046875
- lengths: int32 [6], replicated, may hold values from 1 to 3072, 4096 in all
- page_table: int32 [128, 2], replicated, may hold values from 0 to 15, as said below
Outputs:
- layer_out: bfloat16 [4096, 4096], P(('gx', 'gy'))
- paged_key_value_cache: bfloat16 [128, 2, 32, 1024], P('gx', None, None, 'gy')
Inputs may be any that keep to these rules, and one draw needn't show every extreme that they name: `page_table`: page p belongs to token group p // 16, the tokens of one index of gx. Its owner is an index of gx and its slot is below 16; every pair of owner and slot is taken by exactly one page. Of one token group's pages, 8 owners receive exactly 2 each and the other owners none.
All inputs are finite; a program needn't handle non-finite values.
Results may differ from a plain program's by a relative error of at most 0.025.
The roundings to bfloat16 on the way count: a program that leaves them out, or rounds other values in their place, can miss the bound.
Values may be sent and summed in bfloat16 or wider, within the bound.
A program may use at most 128 MiB of HBM per device.

v0:
```python
import jax
import jax.numpy as jnp
from jax import lax
from jax.sharding import PartitionSpec as P

HEAD_WIDTH = 128
WIN = 4096
PAGE_TOKENS = 32
rope_base = 10000.0
norm_eps = 1e-05
masked_score = -1e30


def partner(value, axis, distance):
    mask = 2**distance
    pairs = [(source, source ^ mask) for source in range(lax.axis_size(axis))]
    return lax.ppermute(value, axis, pairs)


def rms_scale(values, gain):
    floats = values.astype(jnp.float32)
    mean_square = jnp.mean(floats * floats, axis=-1, keepdims=True)
    return floats * lax.rsqrt(mean_square + norm_eps) * gain.astype(jnp.float32)


def segment_info(lengths, token_index):
    ends = jnp.cumsum(lengths, dtype=jnp.int32)
    starts = ends - lengths
    inside = (token_index[:, None] >= starts[None, :]).astype(jnp.int32)
    segment = jnp.sum(inside, axis=1, dtype=jnp.int32) - 1
    chosen = (segment[:, None] == jnp.arange(lengths.shape[0], dtype=jnp.int32)[None, :]).astype(
        jnp.int32
    )
    token_positions = token_index - jnp.sum(chosen * starts[None, :], axis=1, dtype=jnp.int32)
    return (segment, token_positions)


def apply_rotary(values, token_positions):
    half = values.shape[-1] // 2
    freq = rope_base ** (-jnp.arange(half, dtype=jnp.float32) * 2.0 / values.shape[-1])
    angle = token_positions.astype(jnp.float32)[:, None] * freq[None, :]
    cosine = jnp.cos(angle)[:, None, :]
    sine = jnp.sin(angle)[:, None, :]
    first = values[..., :half]
    second = values[..., half:]
    return jnp.concatenate(
        [first * cosine - second * sine, second * cosine + first * sine], axis=-1
    )


def join_halves(mine, other, lower):
    return jnp.where(
        lower, jnp.concatenate([mine, other], axis=1), jnp.concatenate([other, mine], axis=1)
    )


def row_products(source, pieces):
    return tuple((jnp.dot(source, piece, preferred_element_type=jnp.float32) for piece in pieces))


def per_device(
    tokens,
    attn_gain,
    mlp_gain,
    w_query,
    w_key,
    value_projection,
    w_out,
    w_gate,
    w_up,
    w_down,
    lengths,
    page_table,
):
    group_count = lax.axis_size("gx")
    local_rows = tokens.shape[0]
    group = local_rows * lax.axis_size("gy")
    group_index = lax.axis_index("gx")
    head_index = lax.axis_index("gy")
    group_start = group_index * group
    lower = head_index % 2 == 0
    query_cols = w_query.shape[1]
    query_heads = query_cols // HEAD_WIDTH
    key_cols = w_key.shape[1]
    key_heads = max(1, key_cols // HEAD_WIDTH)
    per_key = query_heads // key_heads
    normed = lax.all_gather(
        rms_scale(tokens, attn_gain).astype(jnp.bfloat16), "gy", axis=0, tiled=True
    )
    query = row_products(normed, (lax.all_gather(w_query, "gx", axis=0, tiled=True),))[0]
    key_weight, value_weight = (w_key, value_projection)
    unrotated_key, value_raw = row_products(
        normed,
        (
            lax.all_gather(key_weight, "gx", axis=0, tiled=True),
            lax.all_gather(value_weight, "gx", axis=0, tiled=True),
        ),
    )
    other_key, other_value = (
        partner(unrotated_key.astype(jnp.bfloat16), "gy", 0).astype(unrotated_key.dtype),
        partner(value_raw.astype(jnp.bfloat16), "gy", 0).astype(value_raw.dtype),
    )
    unrotated_key = join_halves(unrotated_key, other_key, lower)
    value_raw = join_halves(value_raw, other_value, lower)
    token_index = group_start + jnp.arange(group, dtype=jnp.int32)
    segment, token_positions = segment_info(lengths, token_index)
    query_rot = (
        apply_rotary(query.reshape(group, query_heads, HEAD_WIDTH), token_positions)
        .astype(jnp.bfloat16)
        .reshape(group, key_heads, per_key, HEAD_WIDTH)
    )
    rotated_key = (
        apply_rotary(unrotated_key.reshape(group, key_heads, HEAD_WIDTH), token_positions)
        .astype(jnp.bfloat16)
        .reshape(group, key_heads * HEAD_WIDTH)
    )
    value_vectors = value_raw.astype(jnp.bfloat16)
    scale = HEAD_WIDTH ** (-0.5)
    start_state = (
        jnp.full((key_heads, per_key, group), masked_score, jnp.float32),
        jnp.zeros((key_heads, per_key, group), jnp.float32),
        jnp.zeros((key_heads, per_key, group, HEAD_WIDTH), jnp.float32),
    )
    keys = lax.all_gather(rotated_key, "gx", axis=0, tiled=True)
    values = lax.all_gather(value_vectors, "gx", axis=0, tiled=True)
    count = keys.shape[0]
    key_index = jnp.arange(count, dtype=jnp.int32)
    key_segment, unused = segment_info(lengths, key_index)
    distance = token_index[:, None] - key_index[None, :]
    allowed = (segment[:, None] == key_segment[None, :]) & (distance >= 0) & (distance < WIN)

    def update(state):
        running, total, weighted = state
        scores = (
            jnp.einsum(
                "qhgd,khd->hgqk",
                query_rot,
                keys.reshape(count, key_heads, HEAD_WIDTH),
                preferred_element_type=jnp.float32,
            )
            * scale
        )
        masked = jnp.where(allowed[None, None], scores, masked_score)
        newest = jnp.maximum(running, jnp.max(masked, axis=-1))
        weights = jnp.where(allowed[None, None], jnp.exp(masked - newest[..., None]), 0.0)
        mixed = jnp.einsum(
            "hgqk,khd->hgqd",
            weights.astype(jnp.bfloat16),
            values.reshape(count, key_heads, HEAD_WIDTH),
            preferred_element_type=jnp.float32,
        )
        return (newest, jnp.sum(weights, axis=-1), mixed)

    state = lax.cond(jnp.any(allowed), update, lambda state: state, start_state)
    attended = (state[2] / state[1][..., None]).astype(jnp.bfloat16)
    attended = attended.transpose(2, 0, 1, 3).reshape(group, query_cols)
    partial_value = jnp.dot(
        attended,
        lax.all_gather(w_out, "gx", axis=1, tiled=True),
        preferred_element_type=jnp.float32,
    )
    share = lax.psum_scatter(
        partial_value.astype(jnp.bfloat16), "gy", scatter_dimension=0, tiled=True
    ).astype(jnp.float32)
    residual = (tokens.astype(jnp.float32) + share).astype(jnp.bfloat16)
    mlp_input = lax.all_gather(
        rms_scale(residual, mlp_gain).astype(jnp.bfloat16), "gy", axis=0, tiled=True
    )
    gate, up_values = row_products(
        mlp_input,
        (
            lax.all_gather(w_gate, "gx", axis=0, tiled=True),
            lax.all_gather(w_up, "gx", axis=0, tiled=True),
        ),
    )
    hidden = (jax.nn.silu(gate) * up_values).astype(jnp.bfloat16)
    down_full = lax.all_gather(w_down, "gx", axis=1, tiled=True)
    mlp_share = lax.psum_scatter(
        jnp.dot(hidden, down_full, preferred_element_type=jnp.float32).astype(jnp.bfloat16),
        "gy",
        scatter_dimension=0,
        tiled=True,
    ).astype(jnp.float32)
    layer_out = (residual.astype(jnp.float32) + mlp_share).astype(jnp.bfloat16)
    own_start = jnp.where(lower, 0, key_cols).astype(jnp.int32)
    local_key = lax.dynamic_slice_in_dim(rotated_key, own_start, key_cols, 1)
    own_value = lax.dynamic_slice_in_dim(value_vectors, own_start, key_cols, 1)
    slots_group = group // PAGE_TOKENS
    capacity = max(2, slots_group // group_count)
    pages_local = (
        jnp.stack([local_key, own_value], axis=0)
        .reshape(2, slots_group, PAGE_TOKENS, key_cols)
        .transpose(1, 0, 2, 3)
        .reshape(slots_group, 2 * PAGE_TOKENS * key_cols)
    )
    owner = page_table[:, 0]
    slot = page_table[:, 1]
    page_index = jnp.arange(owner.shape[0], dtype=jnp.int32)
    page_group = page_index // slots_group
    before = (
        (page_group[:, None] == page_group[None, :])
        & (owner[:, None] == owner[None, :])
        & (page_index[None, :] < page_index[:, None])
    )
    rank = jnp.sum(before.astype(jnp.int32), axis=1, dtype=jnp.int32)
    my_owner = lax.dynamic_slice_in_dim(owner, group_index * slots_group, slots_group, 0)
    my_rank = lax.dynamic_slice_in_dim(rank, group_index * slots_group, slots_group, 0)
    target = jnp.arange(group_count * capacity, dtype=jnp.int32)
    select = (
        (my_owner[None, :] == target[:, None] // capacity)
        & (my_rank[None, :] == target[:, None] % capacity)
    ).astype(jnp.bfloat16)
    outgoing = (
        jnp.dot(select, pages_local, preferred_element_type=jnp.float32)
        .astype(jnp.bfloat16)
        .reshape(group_count, capacity, 2, PAGE_TOKENS, key_cols)
    )
    incoming = lax.all_to_all(outgoing, "gx", split_axis=0, concat_axis=0, tiled=True)
    column = page_group * capacity + rank
    pick = (
        (owner[None, :] == group_index)
        & (slot[None, :] == jnp.arange(slots_group, dtype=jnp.int32)[:, None])
    ).astype(jnp.float32)
    place = (column[:, None] == target[None, :]).astype(jnp.float32)
    routing = jnp.dot(pick, place, preferred_element_type=jnp.float32).astype(jnp.bfloat16)
    paged_key_value_cache = (
        jnp.dot(
            routing,
            incoming.reshape(group_count * capacity, 2 * PAGE_TOKENS * key_cols),
            preferred_element_type=jnp.float32,
        )
        .astype(jnp.bfloat16)
        .reshape(slots_group, 2, PAGE_TOKENS, key_cols)
    )
    return (layer_out, paged_key_value_cache)


def solution(mesh):
    placed = (
        P(("gx", "gy"), None),
        P(),
        P(),
        P("gx", "gy"),
        P("gx", "gy"),
        P("gx", "gy"),
        P("gy", "gx"),
        P("gx", "gy"),
        P("gx", "gy"),
        P("gy", "gx"),
        P(),
        P(),
    )
    return jax.shard_map(
        per_device,
        mesh=mesh,
        in_specs=placed,
        out_specs=(P(("gx", "gy"), None), P("gx", None, None, "gy")),
        check_vma=False,
    )
```

profile of v0, /device:TPU:0, one launch (start us, length us, event | category | flops | bytes accessed | tf_op | source)
XLA Modules:
  0.0 550.2 jit_solution(15981981439846609788)
XLA Ops:
  7.2 0.7 convert_element_type.115
  7.9 1.1 fusion.21
  9.1 1.8 fusion.23
  10.9 0.7 all-gather.12.cloned.1.call-update
  11.7 0.8 reduce-window.9
  12.5 0.7 bitcast_subtract_fusion
  13.4 14.6 %all_gather.35 = bf16[4096,64]{0,1:T(8,128)(2,1)S(1)} all-gather(bf16[512,64]{0,1:T(8,128)(2,1)} %param.18), channel_id=1, replica_groups=mesh['gx'=8,'gy'=16] {'gx'}, dimensions={0}, use_global_device_ids=true | all-gather | bytes 589824 | tf_op jit(solution)/shard_map/all_gather | solution.py:95
  28.0 36.9 %all-gather.10.cloned.1.call-done = bf16[512,4096]{1,0:T(8,128)(2,1)} async-done(((bf16[32,4096]{1,0:T(8,128)(2,1)}), bf16[512,4096]{1,0:T(8,128)(2,1)}) %all-gather.10.cloned.1.call-update) | async-done | bytes 4194320 | tf_op jit(solution)/shard_map/all_gather | solution.py:87
  64.9 3.6 fusion.62
  68.5 1.5 collective-permute-start
  70.0 2.8 collective-permute-done
  72.9 0.6 fusion.37
  73.4 0.7 pad_maximum_fusion.1
  74.2 14.2 %all_gather.37 = bf16[4096,64]{0,1:T(8,128)(2,1)S(1)} all-gather(bf16[512,64]{0,1:T(8,128)(2,1)S(1)} %copy-done.3), channel_id=1, replica_groups=mesh['gx'=8,'gy'=16] {'gx'}, dimensions={0}, use_global_device_ids=true | all-gather | bytes 589824 | tf_op jit(solution)/shard_map/all_gather | solution.py:96
  88.3 3.7 fusion.64
  92.0 1.8 collective-permute-start.1
  93.8 2.6 collective-permute-done.1
  96.4 0.7 fusion.31
  97.9 3.6 fusion.20
  102.1 1.8 multiply_cosine_fusion
  103.9 4.2 fusion.63
  108.5 1.2 fusion.29
  109.9 7.8 %all-gather.14.cloned.1.call-done = bf16[4096,128]{0,1:T(8,128)(2,1)} async-done(((bf16[512,128]{0,1:T(8,128)(2,1)}), bf16[4096,128]{0,1:T(8,128)(2,1)}) %all-gather.14.cloned.1.call-update) | async-done | bytes 1048592 | tf_op jit(solution)/shard_map/all_gather | solution.py:124
  117.7 25.0 %all-gather.16.cloned.1.call-done = bf16[4096,128]{0,1:T(8,128)(2,1)} async-done(((bf16[512,128]{0,1:T(8,128)(2,1)}), bf16[4096,128]{0,1:T(8,128)(2,1)}) %all-gather.16.cloned.1.call-update) | async-done | bytes 1048592 | tf_op jit(solution)/shard_map/all_gather | solution.py:125
  142.8 14.2 %conditional.1 = (f32[1,2,512]{2,1,0:T(2,128)S(1)}, f32[1,2,512,128]{2,3,1,0:T(8,128)S(1)}) conditional(s32[]{:T(128)} %convert_element_type.114, () %tuple.16, (pred[512,4096]{0,1:T(8,128)(4,1)S(1)}, bf16[512,1,2,128]{3,0,2,1:T(8,128)(2,1)S(1)}, bf16[4096,128]{0,1:T(8,128)(2,1)}, bf16[4096,128]{0,1:T(8,128)(2,1)}) %tuple.17), branch_computations={%region_6.7_spmd, %region_7.10_spmd} | conditional | flops 2202008576 | bytes 63725612 | solution.py:154
  142.8 5.1 fusion
  147.9 4.6 fusion.7
  152.5 4.4 fusion.2
  157.0 12.6 %all-gather.18.cloned.1.call-done = bf16[256,4096]{1,0:T(8,128)(2,1)} async-done(((bf16[256,512]{1,0:T(8,128)(2,1)}), bf16[256,4096]{1,0:T(8,128)(2,1)}) %all-gather.18.cloned.1.call-update) | async-done | bytes 2097168 | tf_op jit(solution)/shard_map/all_gather | solution.py:159
  169.6 4.9 convolution_convert_fusion.1
  174.6 0.7 all-gather.22.cloned.1.call-update
  175.4 77.2 %reduce-scatter.3.cloned.1.call-done = bf16[32,4096]{1,0:T(8,128)(2,1)} async-done(((bf16[512,4096]{1,0:T(8,128)(2,1)}), bf16[32,4096]{1,0:T(8,128)(2,1)}) %reduce-scatter.3.cloned.1.call-update) | async-done | bytes 262160 | tf_op jit(solution)/shard_map/reduce_scatter | solution.py:162
  252.6 1.1 fusion.25
  253.7 1.8 fusion.27
  255.6 0.7 all-gather.24.cloned.1.call-update
  257.1 42.2 %all-gather.22.cloned.1.call-done = bf16[4096,896]{1,0:T(8,128)(2,1)} async-done(((bf16[512,896]{1,0:T(8,128)(2,1)}), bf16[4096,896]{1,0:T(8,128)(2,1)}) %all-gather.22.cloned.1.call-update) | async-done | bytes 7340048 | tf_op jit(solution)/shard_map/all_gather | solution.py:172
  299.4 54.3 %all-gather.20.cloned.1.call-done = bf16[512,4096]{1,0:T(8,128)(2,1)} async-done(((bf16[32,4096]{1,0:T(8,128)(2,1)}), bf16[512,4096]{1,0:T(8,128)(2,1)}) %all-gather.20.cloned.1.call-update) | async-done | bytes 4194320 | tf_op jit(solution)/shard_map/all_gather | solution.py:166
  353.7 9.8 %fusion.65 = f32[512,896]{1,0:T(8,128)S(1)} fusion(bf16[512,4096]{1,0:T(8,128)(2,1)} %all-gather.20.cloned.1.call-done, bf16[4096,896]{1,0:T(8,128)(2,1)} %all-gather.22.cloned.1.call-done), kind=kOutput, calls=%fused_computation.120 | convolution fusion | flops 3758096384 | bytes 13369344 | tf_op jit(solution)/shard_map/dot_general | solution.py:58
  363.5 37.2 %all-gather.24.cloned.1.call-done = bf16[4096,896]{1,0:T(8,128)(2,1)} async-done(((bf16[512,896]{1,0:T(8,128)(2,1)}), bf16[4096,896]{1,0:T(8,128)(2,1)}) %all-gather.24.cloned.1.call-update) | async-done | bytes 7340048 | tf_op jit(solution)/shard_map/all_gather | solution.py:173
  400.8 47.2 %all-gather.26.cloned.1.call-done = bf16[896,4096]{1,0:T(8,128)(2,1)} async-done(((bf16[896,512]{1,0:T(8,128)(2,1)}), bf16[896,4096]{1,0:T(8,128)(2,1)}) %all-gather.26.cloned.1.call-update) | async-done | bytes 7340048 | tf_op jit(solution)/shard_map/all_gather | solution.py:177
  448.0 16.3 %convolution_convert_fusion = bf16[512,4096]{1,0:T(8,128)(2,1)} fusion(bf16[896,4096]{1,0:T(8,128)(2,1)} %all-gather.26.cloned.1.call-done, f32[512,896]{1,0:T(8,128)S(1)} %fusion.65, bf16[512,4096]{1,0:T(8,128)(2,1)} %all-gather.20.cloned.1.call-done, bf16[4096,896]{1,0:T(8,128)(2,1)} %all-gather.24.cloned.1.call-done), kind=kOutput, calls=%fused_computation.22 | convolution fusion | flops 7521042432 | bytes 24903680 | tf_op jit(solution)/shard_map/dot_general | solution.py:179
  464.3 0.6 copy-done.5
  466.5 0.9 reshape.453
  467.4 3.4 all-to-all-start
  470.7 6.0 %all-to-all-done = bf16[8,2,4096]{2,1,0:T(2,128)(2,1)S(1)} async-done(((bf16[8,2,4096]{2,1,0:T(2,128)(2,1)}), bf16[8,2,4096]{2,1,0:T(2,128)(2,1)S(1)}, u32[]{:S(2)}, u32[]{:S(2)}) %all-to-all-start) | async-done | bytes 131104 | tf_op jit(solution)/shard_map/all_to_all | solution.py:218
  477.7 1.0 reshape.449
  478.6 63.3 %reduce-scatter.5.cloned.1.call-done = bf16[32,4096]{1,0:T(8,128)(2,1)} async-done(((bf16[512,4096]{1,0:T(8,128)(2,1)}), bf16[32,4096]{1,0:T(8,128)(2,1)}) %reduce-scatter.5.cloned.1.call-update) | async-done | bytes 262160 | tf_op jit(solution)/shard_map/reduce_scatter | solution.py:178
  541.9 1.7 fusion.28
  (72 shorter events, 5.2 us)
Async XLA Ops:
  7.2 57.7 %all-gather.10.cloned.1.call-start = ((), (), s32[]{:S(2)}) async-start(), calls=%async_computation.3 | async-start | bytes 4456448 | tf_op jit(solution)/shard_map/all_gather | solution.py:87
  7.9 66.3 %copy-start.3 = (bf16[512,64]{0,1:T(8,128)(2,1)S(1)}, bf16[512,64]{0,1:T(8,128)(2,1)}, u32[]{:S(2)}) copy-start(bf16[512,64]{0,1:T(8,128)(2,1)} %param.19) | copy-start | bytes 196612
  10.9 93.0 %all-gather.12.cloned.1.call-start = ((), (), s32[]{:S(2)}) async-start(), calls=%async_computation.4 | async-start | bytes 2359296 | tf_op jit(solution)/shard_map/all_gather | solution.py:90
  11.6 106.1 %all-gather.14.cloned.1.call-start = ((), (), s32[]{:S(2)}) async-start(), calls=%async_computation.5 | async-start | bytes 1179648 | tf_op jit(solution)/shard_map/all_gather | solution.py:124
  68.5 4.3 collective-permute-start
  74.1 68.7 %all-gather.16.cloned.1.call-start = ((), (), s32[]{:S(2)}) async-start(), calls=%async_computation.6 | async-start | bytes 1179648 | tf_op jit(solution)/shard_map/all_gather | solution.py:125
  92.0 4.4 collective-permute-start.1
  97.1 72.5 %all-gather.18.cloned.1.call-start = ((), (), s32[]{:S(2)}) async-start(), calls=%async_computation.7 | async-start | bytes 2359296 | tf_op jit(solution)/shard_map/all_gather | solution.py:159
  97.7 154.9 %reduce-scatter.3.cloned.1.call-start = ((), (), s32[]{:S(2)}) async-start(), calls=%async_computation.8 | async-start | bytes 4456448 | tf_op jit(solution)/shard_map/reduce_scatter | solution.py:162
  142.8 5.2 copy-start.6
  174.6 0.8 copy-start.4
  174.6 78.0 %copy-start = (bf16[32,4096]{1,0:T(8,128)(2,1)S(1)}, bf16[32,4096]{1,0:T(8,128)(2,1)}, u32[]{:S(2)}) copy-start(bf16[32,4096]{1,0:T(8,128)(2,1)} %param.14) | copy-start | bytes 786436
  174.6 124.8 %all-gather.22.cloned.1.call-start = ((), (), s32[]{:S(2)}) async-start(), calls=%async_computation.10 | async-start | bytes 8257536 | tf_op jit(solution)/shard_map/all_gather | solution.py:172
  175.3 178.4 %all-gather.20.cloned.1.call-start = ((), (), s32[]{:S(2)}) async-start(), calls=%async_computation.9 | async-start | bytes 4456448 | tf_op jit(solution)/shard_map/all_gather | solution.py:166
  255.5 145.2 %all-gather.24.cloned.1.call-start = ((), (), s32[]{:S(2)}) async-start(), calls=%async_computation.11 | async-start | bytes 8257536 | tf_op jit(solution)/shard_map/all_gather | solution.py:173
  256.3 191.7 %all-gather.26.cloned.1.call-start = ((), (), s32[]{:S(2)}) async-start(), calls=%async_computation.12 | async-start | bytes 8257536 | tf_op jit(solution)/shard_map/all_gather | solution.py:177
  256.9 285.0 %reduce-scatter.5.cloned.1.call-start = ((), (), s32[]{:S(2)}) async-start(), calls=%async_computation.13 | async-start | bytes 4456448 | tf_op jit(solution)/shard_map/reduce_scatter | solution.py:178
  464.2 0.7 copy-start.5
  464.2 1.2 copy-start.2
  464.2 77.7 %copy-start.1 = (bf16[32,4096]{1,0:T(8,128)(2,1)S(1)}, bf16[32,4096]{1,0:T(8,128)(2,1)}, u32[]{:S(2)}) copy-start(bf16[32,4096]{1,0:T(8,128)(2,1)} %reduce-scatter.3.cloned.1.call-done) | copy-start | bytes 786436
  467.4 9.4 %all-to-all-start = ((bf16[8,2,4096]{2,1,0:T(2,128)(2,1)}), bf16[8,2,4096]{2,1,0:T(2,128)(2,1)S(1)}, u32[]{:S(2)}, u32[]{:S(2)}) async-start(bf16[8,2,4096]{2,1,0:T(2,128)(2,1)} %reshape.453), calls=%async_computation.2 | async-start | bytes 262144 | tf_op jit(solution)/shard_map/all_to_all | solution.py:218
Sparse Core Ops, SparseCore 0:
  11.0 53.8 all-gather.9
  66.6 25.7 all-gather.11
  94.1 23.5 all-gather.13
  119.3 23.4 all-gather.15
  144.3 25.2 all-gather.17
  174.7 77.8 reduce-scatter.2
  254.4 44.9 all-gather.21
  302.3 51.3 all-gather.19
  355.5 45.2 all-gather.23
  402.4 45.4 all-gather.25
  464.4 77.4 reduce-scatter.4
where the time goes:
time: 551 us; the launch traced here: 550 us
  waiting for transfers between devices  419 us (76%)
  matrix products  52.7 us (10%)
  blocking collectives  28.8 us (5%)
  other arithmetic  23.6 us (4%)
  between operations  14.8 us (3%)
  starting transfers between devices  7.29 us (1%)
    reduce_scatter x1, waiting for transfers between devices, per_device(): lax.psum_scatter(partial_value.astype(jnp.bfloat16), 'gy', scatter_dimens...  77.2 us
    reduce_scatter x1, waiting for transfers between devices, per_device(): lax.psum_scatter(jnp.dot(hidden, down_full, preferred_element_type=jnp.fl...  63.3 us
    all_gather x1, waiting for transfers between devices, per_device(): lax.all_gather(rms_scale(residual, mlp_gain).astype(jnp.bfloat16), 'gy',...  54.3 us
    all_gather x1, waiting for transfers between devices, per_device(): down_full = lax.all_gather(w_down, 'gx', axis=1, tiled=True)  47.2 us
    all_gather x1, waiting for transfers between devices, per_device(): lax.all_gather(w_gate, 'gx', axis=0, tiled=True)  42.2 us
    all_gather x1, waiting for transfers between devices, per_device(): lax.all_gather(w_up, 'gx', axis=0, tiled=True)  37.2 us
    all_gather x1, waiting for transfers between devices, per_device(): lax.all_gather(rms_scale(tokens, attn_gain).astype(jnp.bfloat16), 'gy', a...  36.9 us
    all_gather x1, waiting for transfers between devices, per_device(): values = lax.all_gather(value_vectors, 'gx', axis=0, tiled=True)  25 us
  transfers between devices with their start and end apart: 14, of which 13 were waited for; matrix products, arithmetic and copies ran while one was open for 10% of the time, Pallas kernels for 0%

commit v1 on v0

--- a/solution.py
+++ b/solution.py
@@ -122,7 +122,13 @@
         jnp.zeros((key_heads, per_key, group, HEAD_WIDTH), jnp.float32),
     )
     keys = lax.all_gather(rotated_key, "gx", axis=0, tiled=True)
-    values = lax.all_gather(value_vectors, "gx", axis=0, tiled=True)
+    size = lax.axis_size("gx")
+    block, blocks = (value_vectors, [value_vectors])
+    for _ in range(size - 1):
+        block = lax.ppermute(block, "gx", [(i, (i + 1) % size) for i in range(size)])
+        blocks.insert(0, block)
+    line = jnp.concatenate(blocks, axis=0)
+    values = jnp.roll(line, (lax.axis_index("gx") + 1) * value_vectors.shape[0], axis=0)
     count = keys.shape[0]
     key_index = jnp.arange(count, dtype=jnp.int32)
     key_segment, unused = segment_info(lengths, key_index)

time: 551 us -> 562 us (1.020)
  local copies, waits for them, and re-layouts: 4.37 us -> 25.9 us
  waiting for transfers between devices: 419 us -> 401 us
  matrix products: 52.7 us -> 59.9 us
    ppermute x0 -> x7, waiting for transfers between devices: none -> 31.8 us  [per_device(): lax.ppermute(block, 'gx', [(i, (i + 1) % size) for i in range(size)])]
    all_gather x1 -> x0, waiting for transfers between devices: 25 us -> none  [per_device(): values = lax.all_gather(value_vectors, 'gx', axis=0, tiled=True)]
    unnamed x16 -> x53, local copies, waits for them, and re-layouts: 2.16 us -> 16.6 us
    all_gather x1, waiting for transfers between devices: 12.6 us -> 0.02 us  [per_device(): lax.all_gather(w_out, 'gx', axis=1, tiled=True)]
    all_gather x1, waiting for transfers between devices: 7.85 us -> 0.01 us  [per_device(): keys = lax.all_gather(rotated_key, 'gx', axis=0, tiled=True)]
  transfers between devices with their start and end apart: 14 -> 20, of which waited for: 13 -> 17; matrix products, arithmetic and copies ran while one was open for 10% -> 14% of each run, Pallas kernels for 0% -> 0%
where the time goes in v1:
time: 562 us; the launch traced here: 561 us
  waiting for transfers between devices  401 us (71%)
  matrix products  59.9 us (11%)
  blocking collectives  28.9 us (5%)
  local copies, waits for them, and re-layouts  25.9 us (5%)
  other arithmetic  22.9 us (4%)
  between operations  15.2 us (3%)
  starting transfers between devices  7.02 us (1%)
    reduce_scatter x1, waiting for transfers between devices, per_device(): lax.psum_scatter(partial_value.astype(jnp.bfloat16), 'gy', scatter_dimens...  73.6 us
    reduce_scatter x1, waiting for transfers between devices, per_device(): lax.psum_scatter(jnp.dot(hidden, down_full, preferred_element_type=jnp.fl...  63.3 us
    all_gather x1, waiting for transfers between devices, per_device(): lax.all_gather(rms_scale(residual, mlp_gain).astype(jnp.bfloat16), 'gy',...  54.3 us
    all_gather x1, waiting for transfers between devices, per_device(): down_full = lax.all_gather(w_down, 'gx', axis=1, tiled=True)  47.3 us
    all_gather x1, waiting for transfers between devices, per_device(): lax.all_gather(w_gate, 'gx', axis=0, tiled=True)  41.9 us
    all_gather x1, waiting for transfers between devices, per_device(): lax.all_gather(w_up, 'gx', axis=0, tiled=True)  37.3 us
    all_gather x1, waiting for transfers between devices, per_device(): lax.all_gather(rms_scale(tokens, attn_gain).astype(jnp.bfloat16), 'gy', a...  36.9 us
    ppermute x7, waiting for transfers between devices, per_device(): lax.ppermute(block, 'gx', [(i, (i + 1) % size) for i in range(size)])  31.8 us
  transfers between devices with their start and end apart: 20, of which 17 were waited for; matrix products, arithmetic and copies ran while one was open for 14% of the time, Pallas kernels for 0%

profile of v1, /device:TPU:0, one launch (start us, length us, event | category | flops | bytes accessed | tf_op | source)
XLA Modules:
  0.0 560.9 jit_solution(11295659468666818398)
XLA Ops:
  7.9 1.1 fusion.23
  9.0 1.8 fusion.25
  13.3 14.6 %all_gather.32 = bf16[4096,64]{0,1:T(8,128)(2,1)S(1)} all-gather(bf16[512,64]{0,1:T(8,128)(2,1)} %param.18), channel_id=1, replica_groups=mesh['gx'=8,'gy'=16] {'gx'}, dimensions={0}, use_global_device_ids=true | all-gather | bytes 589824 | tf_op jit(solution)/shard_map/all_gather | solution.py:95
  27.9 36.9 %all-gather.9.cloned.1.call-done = bf16[512,4096]{1,0:T(8,128)(2,1)} async-done(((bf16[32,4096]{1,0:T(8,128)(2,1)}), bf16[512,4096]{1,0:T(8,128)(2,1)}) %all-gather.9.cloned.1.call-update) | async-done | bytes 4194320 | tf_op jit(solution)/shard_map/all_gather | solution.py:87
  64.9 3.6 fusion.64
  68.4 1.5 collective-permute-start
  70.0 2.8 collective-permute-done
  74.8 14.3 %all_gather.34 = bf16[4096,64]{0,1:T(8,128)(2,1)S(1)} all-gather(bf16[512,64]{0,1:T(8,128)(2,1)S(1)} %copy-done.15), channel_id=1, replica_groups=mesh['gx'=8,'gy'=16] {'gx'}, dimensions={0}, use_global_device_ids=true | all-gather | bytes 589824 | tf_op jit(solution)/shard_map/all_gather | solution.py:96
  89.1 3.6 fusion.66
  92.7 1.5 collective-permute-start.1
  94.2 2.9 collective-permute-done.1
  97.3 5.4 collective-permute-done.2
  102.8 6.6 %collective-permute-done.3 = bf16[512,128]{0,1:T(8,128)(2,1)S(1)} collective-permute-done((bf16[512,128]{0,1:T(8,128)(2,1)S(1)}, bf16[512,128]{0,1:T(8,128)(2,1)S(1)}, u32[]{:S(2)}, u32[]{:S(2)}) %collective-permute-start.3) | collective-permute-done | bytes 131104 | tf_op jit(solution)/shard_map/ppermute | solution.py:128
  109.4 3.6 fusion.22
  113.6 1.9 collective-permute-done.4
  115.5 1.8 multiply_cosine_fusion
  117.4 3.8 collective-permute-done.5
  121.2 4.2 fusion.65
  125.4 1.5 collective-permute-done.6
  127.3 5.4 collective-permute-done.7
  132.8 1.2 fusion.31
  134.2 7.1 %collective-permute-done.8 = bf16[512,128]{0,1:T(8,128)(2,1)S(1)} collective-permute-done((bf16[512,128]{0,1:T(8,128)(2,1)}, bf16[512,128]{0,1:T(8,128)(2,1)S(1)}, u32[]{:S(2)}, u32[]{:S(2)}) %collective-permute-start.8) | collective-permute-done | bytes 131104 | tf_op jit(solution)/shard_map/ppermute | solution.py:128
  142.0 1.6 constant_dynamic-update-slice_fusion.14
  143.5 1.6 constant_dynamic-update-slice_fusion.13
  149.2 1.6 constant_dynamic-update-slice_fusion.6
  150.8 1.6 constant_dynamic-update-slice_fusion.5
  155.7 27.9 %conditional.1 = (f32[1,2,512]{2,1,0:T(2,128)S(1)}, f32[1,2,512,128]{2,3,1,0:T(8,128)S(1)}) conditional(s32[]{:T(128)} %convert_element_type.117, () %tuple.24, (pred[512,4096]{0,1:T(8,128)(4,1)S(1)}, bf16[512,1,2,128]{3,0,2,1:T(8,128)(2,1)S(1)}, bf16[4096,128]{0,1:T(8,128)(2,1)}, s32[]{:T(128)}, s32[]{:T(128)}, ...), branch_computations={%region_6.7_spmd, %region_7.10_spmd.clone} | conditional | flops 2202008576 | bytes 130834624 | solution.py:160
  155.7 8.6 %fusion = (f32[2,512]{1,0:T(2,128)S(1)}, f32[4096,512,2]{1,0,2:T(8,128)}) fusion(pred[512,4096]{0,1:T(8,128)(4,1)S(1)} %get-tuple-element.113, bf16[512,1,2,128]{3,0,2,1:T(8,128)(2,1)S(1)} %get-tuple-element.115, bf16[4096,128]{0,1:T(8,128)(2,1)} %get-tuple-element.147), kind=kOutput, calls=%fused_computation.2 | convolution fusion | flops 1086323712 | bytes 20189184 | tf_op jit(solution)/shard_map/cond/branch_1_fun/qhgd,khd->hgqk/dot_general | solution.py:141
  164.3 4.1 copy.32
  168.4 8.5 %fusion.7 = f32[1,2,512,128]{2,3,1,0:T(8,128)S(1)} fusion(f32[4096,512,2]{1,0,2:T(8,128)} %get-tuple-element.157, f32[2,512]{1,0:T(2,128)S(1)} %broadcast_maximum_fusion, pred[512,4096]{0,1:T(8,128)(4,1)S(1)} %get-tuple-element.113, bf16[8192,128]{1,0:T(8,128)(2,1)} %copy.32, s32[]{:T(128)S(6)} %select_n.122), kind=kOutput, calls=%fused_computation.8 | convolution fusion | flops 1094713344 | bytes 20451332 | tf_op jit(solution)/shard_map/cond/branch_1_fun/hgqk,khd->hgqd/dot_general | solution.py:152
  176.8 2.4 copy-done
  179.2 4.4 fusion.2
  183.7 4.9 convolution_convert_fusion.1
  189.3 73.6 %reduce-scatter.3.cloned.1.call-done = bf16[32,4096]{1,0:T(8,128)(2,1)} async-done(((bf16[512,4096]{1,0:T(8,128)(2,1)}), bf16[32,4096]{1,0:T(8,128)(2,1)}) %reduce-scatter.3.cloned.1.call-update) | async-done | bytes 262160 | tf_op jit(solution)/shard_map/reduce_scatter | solution.py:168
  262.9 1.1 fusion.27
  264.0 1.8 fusion.29
  267.6 41.9 %all-gather.19.cloned.1.call-done = bf16[4096,896]{1,0:T(8,128)(2,1)} async-done(((bf16[512,896]{1,0:T(8,128)(2,1)}), bf16[4096,896]{1,0:T(8,128)(2,1)}) %all-gather.19.cloned.1.call-update) | async-done | bytes 7340048 | tf_op jit(solution)/shard_map/all_gather | solution.py:178
  309.5 54.3 %all-gather.17.cloned.1.call-done = bf16[512,4096]{1,0:T(8,128)(2,1)} async-done(((bf16[32,4096]{1,0:T(8,128)(2,1)}), bf16[512,4096]{1,0:T(8,128)(2,1)}) %all-gather.17.cloned.1.call-update) | async-done | bytes 4194320 | tf_op jit(solution)/shard_map/all_gather | solution.py:172
  363.9 9.8 %fusion.67 = f32[512,896]{1,0:T(8,128)S(1)} fusion(bf16[512,4096]{1,0:T(8,128)(2,1)} %all-gather.17.cloned.1.call-done, bf16[4096,896]{1,0:T(8,128)(2,1)} %all-gather.19.cloned.1.call-done), kind=kOutput, calls=%fused_computation.138 | convolution fusion | flops 3758096384 | bytes 13369344 | tf_op jit(solution)/shard_map/dot_general | solution.py:58
  373.7 37.3 %all-gather.21.cloned.1.call-done = bf16[4096,896]{1,0:T(8,128)(2,1)} async-done(((bf16[512,896]{1,0:T(8,128)(2,1)}), bf16[4096,896]{1,0:T(8,128)(2,1)}) %all-gather.21.cloned.1.call-update) | async-done | bytes 7340048 | tf_op jit(solution)/shard_map/all_gather | solution.py:179
  410.9 47.3 %all-gather.23.cloned.1.call-done = bf16[896,4096]{1,0:T(8,128)(2,1)} async-done(((bf16[896,512]{1,0:T(8,128)(2,1)}), bf16[896,4096]{1,0:T(8,128)(2,1)}) %all-gather.23.cloned.1.call-update) | async-done | bytes 7340048 | tf_op jit(solution)/shard_map/all_gather | solution.py:183
  458.3 16.3 %convolution_convert_fusion = bf16[512,4096]{1,0:T(8,128)(2,1)} fusion(bf16[896,4096]{1,0:T(8,128)(2,1)} %all-gather.23.cloned.1.call-done, f32[512,896]{1,0:T(8,128)S(1)} %fusion.67, bf16[512,4096]{1,0:T(8,128)(2,1)} %all-gather.17.cloned.1.call-done, bf16[4096,896]{1,0:T(8,128)(2,1)} %all-gather.21.cloned.1.call-done), kind=kOutput, calls=%fused_computation.24 | convolution fusion | flops 7521042432 | bytes 24903680 | tf_op jit(solution)/shard_map/dot_general | solution.py:185
  476.8 0.9 reshape.472
  477.7 3.4 all-to-all-start
  481.1 6.0 %all-to-all-done = bf16[8,2,4096]{2,1,0:T(2,128)(2,1)S(1)} async-done(((bf16[8,2,4096]{2,1,0:T(2,128)(2,1)}), bf16[8,2,4096]{2,1,0:T(2,128)(2,1)S(1)}, u32[]{:S(2)}, u32[]{:S(2)}) %all-to-all-start) | async-done | bytes 131104 | tf_op jit(solution)/shard_map/all_to_all | solution.py:224
  488.0 1.0 reshape.466
  489.0 63.3 %reduce-scatter.5.cloned.1.call-done = bf16[32,4096]{1,0:T(8,128)(2,1)} async-done(((bf16[512,4096]{1,0:T(8,128)(2,1)}), bf16[32,4096]{1,0:T(8,128)(2,1)}) %reduce-scatter.5.cloned.1.call-update) | async-done | bytes 262160 | tf_op jit(solution)/shard_map/reduce_scatter | solution.py:184
  552.3 1.7 fusion.30
  (122 shorter events, 19.6 us)
Async XLA Ops:
  7.2 57.7 %all-gather.9.cloned.1.call-start = ((), (), s32[]{:S(2)}) async-start(), calls=%async_computation.3 | async-start | bytes 4456448 | tf_op jit(solution)/shard_map/all_gather | solution.py:87
  10.8 110.3 %all-gather.11.cloned.1.call-start = ((), (), s32[]{:S(2)}) async-start(), calls=%async_computation.4 | async-start | bytes 2359296 | tf_op jit(solution)/shard_map/all_gather | solution.py:90
  11.6 144.1 %all-gather.13.cloned.1.call-start = ((), (), s32[]{:S(2)}) async-start(), calls=%async_computation.5 | async-start | bytes 1179648 | tf_op jit(solution)/shard_map/all_gather | solution.py:124
  27.9 46.9 %copy-start.15 = (bf16[512,64]{0,1:T(8,128)(2,1)S(1)}, bf16[512,64]{0,1:T(8,128)(2,1)}, u32[]{:S(2)}) copy-start(bf16[512,64]{0,1:T(8,128)(2,1)} %param.19) | copy-start | bytes 196612
  68.4 4.3 collective-permute-start
  73.4 0.6 copy-start.3
  73.4 0.7 copy-start.5
  74.7 109.0 %all-gather.15.cloned.1.call-start = ((), (), s32[]{:S(2)}) async-start(), calls=%async_computation.6 | async-start | bytes 2359296 | tf_op jit(solution)/shard_map/all_gather | solution.py:165
  92.7 4.4 collective-permute-start.1
  97.1 5.6 %collective-permute-start.2 = (bf16[512,128]{0,1:T(8,128)(2,1)S(1)}, bf16[512,128]{0,1:T(8,128)(2,1)S(1)}, u32[]{:S(2)}, u32[]{:S(2)}) collective-permute-start(bf16[512,128]{0,1:T(8,128)(2,1)S(1)} %fusion.33), channel_id=1, source_target_pairs={{0,16},{16,32},{32,48},{48,64},{64,80},{80,96},{96,112},{112,0},{1... | collective-permute-start | bytes 393224 | tf_op jit(solution)/shard_map/ppermute | solution.py:128
  97.2 165.7 %reduce-scatter.3.cloned.1.call-start = ((), (), s32[]{:S(2)}) async-start(), calls=%async_computation.7 | async-start | bytes 4456448 | tf_op jit(solution)/shard_map/reduce_scatter | solution.py:168
  102.7 6.7 %copy-start.7 = (bf16[512,128]{0,1:T(8,128)(2,1)}, bf16[512,128]{0,1:T(8,128)(2,1)S(1)}, u32[]{:S(2)}) copy-start(bf16[512,128]{0,1:T(8,128)(2,1)S(1)} %collective-permute-done.2) | copy-start | bytes 393220
  102.7 6.7 %collective-permute-start.3 = (bf16[512,128]{0,1:T(8,128)(2,1)S(1)}, bf16[512,128]{0,1:T(8,128)(2,1)S(1)}, u32[]{:S(2)}, u32[]{:S(2)}) collective-permute-start(bf16[512,128]{0,1:T(8,128)(2,1)S(1)} %collective-permute-done.2), channel_id=1, source_target_pairs={{0,16},{16,32},{32,48},{48,64},{64,80},{80,96},{96,112},{112,0},{1... | collective-permute-start | bytes 393224 | tf_op jit(solution)/shard_map/ppermute | solution.py:128
  109.4 11.7 %copy-start.9 = (bf16[512,128]{0,1:T(8,128)(2,1)}, bf16[512,128]{0,1:T(8,128)(2,1)S(1)}, u32[]{:S(2)}) copy-start(bf16[512,128]{0,1:T(8,128)(2,1)S(1)} %collective-permute-done.3) | copy-start | bytes 393220
  109.4 6.1 %collective-permute-start.4 = (bf16[512,128]{0,1:T(8,128)(2,1)S(1)}, bf16[512,128]{0,1:T(8,128)(2,1)S(1)}, u32[]{:S(2)}, u32[]{:S(2)}) collective-permute-start(bf16[512,128]{0,1:T(8,128)(2,1)S(1)} %collective-permute-done.3), channel_id=1, source_target_pairs={{0,16},{16,32},{32,48},{48,64},{64,80},{80,96},{96,112},{112,0},{1... | collective-permute-start | bytes 393224 | tf_op jit(solution)/shard_map/ppermute | solution.py:128
  115.5 5.6 %copy-start.11 = (bf16[512,128]{0,1:T(8,128)(2,1)}, bf16[512,128]{0,1:T(8,128)(2,1)S(1)}, u32[]{:S(2)}) copy-start(bf16[512,128]{0,1:T(8,128)(2,1)S(1)} %collective-permute-done.4) | copy-start | bytes 393220
  115.5 5.6 collective-permute-start.5
  121.1 4.2 copy-start.13
  121.1 5.7 %collective-permute-start.6 = (bf16[512,128]{0,1:T(8,128)(2,1)S(1)}, bf16[512,128]{0,1:T(8,128)(2,1)}, u32[]{:S(2)}, u32[]{:S(2)}) collective-permute-start(bf16[512,128]{0,1:T(8,128)(2,1)S(1)} %collective-permute-done.5), channel_id=1, source_target_pairs={{0,16},{16,32},{32,48},{48,64},{64,80},{80,96},{96,112},{112,0},{1... | collective-permute-start | bytes 393224 | tf_op jit(solution)/shard_map/ppermute | solution.py:128
  126.9 5.9 %collective-permute-start.7 = (bf16[512,128]{0,1:T(8,128)(2,1)}, bf16[512,128]{0,1:T(8,128)(2,1)}, u32[]{:S(2)}, u32[]{:S(2)}) collective-permute-start(bf16[512,128]{0,1:T(8,128)(2,1)} %collective-permute-done.6), channel_id=1, source_target_pairs={{0,16},{16,32},{32,48},{48,64},{64,80},{80,96},{96,112},{112,0},{1... | collective-permute-start | bytes 393224 | tf_op jit(solution)/shard_map/ppermute | solution.py:128
  127.3 17.8 %copy-start.14 = (bf16[512,128]{0,1:T(8,128)(2,1)S(1)}, bf16[512,128]{0,1:T(8,128)(2,1)}, u32[]{:S(2)}) copy-start(bf16[512,128]{0,1:T(8,128)(2,1)} %copy-done.13) | copy-start | bytes 393220
  127.3 18.5 %copy-start.12 = (bf16[512,128]{0,1:T(8,128)(2,1)S(1)}, bf16[512,128]{0,1:T(8,128)(2,1)}, u32[]{:S(2)}) copy-start(bf16[512,128]{0,1:T(8,128)(2,1)} %copy-done.11) | copy-start | bytes 393220
  132.8 8.5 %collective-permute-start.8 = (bf16[512,128]{0,1:T(8,128)(2,1)}, bf16[512,128]{0,1:T(8,128)(2,1)S(1)}, u32[]{:S(2)}, u32[]{:S(2)}) collective-permute-start(bf16[512,128]{0,1:T(8,128)(2,1)} %collective-permute-done.7), channel_id=1, source_target_pairs={{0,16},{16,32},{32,48},{48,64},{64,80},{80,96},{96,112},{112,0},{1... | collective-permute-start | bytes 393224 | tf_op jit(solution)/shard_map/ppermute | solution.py:128
  132.8 13.7 %copy-start.10 = (bf16[512,128]{0,1:T(8,128)(2,1)S(1)}, bf16[512,128]{0,1:T(8,128)(2,1)}, u32[]{:S(2)}) copy-start(bf16[512,128]{0,1:T(8,128)(2,1)} %copy-done.9) | copy-start | bytes 393220
  132.8 14.4 %copy-start.8 = (bf16[512,128]{0,1:T(8,128)(2,1)S(1)}, bf16[512,128]{0,1:T(8,128)(2,1)}, u32[]{:S(2)}) copy-start(bf16[512,128]{0,1:T(8,128)(2,1)} %copy-done.7) | copy-start | bytes 393220
  168.4 10.8 %copy-start = (f32[4096,512,2]{1,0,2:T(8,128)S(1)}, f32[4096,512,2]{1,0,2:T(8,128)}, u32[]{:S(2)}) copy-start(f32[4096,512,2]{1,0,2:T(8,128)} %get-tuple-element.157) | copy-start | bytes 50331652 | tf_op jit(solution)/shard_map/cond
  188.6 0.7 copy-start.16
  188.6 74.3 %copy-start.1 = (bf16[32,4096]{1,0:T(8,128)(2,1)S(1)}, bf16[32,4096]{1,0:T(8,128)(2,1)}, u32[]{:S(2)}) copy-start(bf16[32,4096]{1,0:T(8,128)(2,1)} %param.14) | copy-start | bytes 786436
  188.7 120.9 %all-gather.19.cloned.1.call-start = ((), (), s32[]{:S(2)}) async-start(), calls=%async_computation.9 | async-start | bytes 8257536 | tf_op jit(solution)/shard_map/all_gather | solution.py:178
  189.2 174.6 %all-gather.17.cloned.1.call-start = ((), (), s32[]{:S(2)}) async-start(), calls=%async_computation.8 | async-start | bytes 4456448 | tf_op jit(solution)/shard_map/all_gather | solution.py:172
  265.8 145.1 %all-gather.21.cloned.1.call-start = ((), (), s32[]{:S(2)}) async-start(), calls=%async_computation.10 | async-start | bytes 8257536 | tf_op jit(solution)/shard_map/all_gather | solution.py:179
  266.6 191.7 %all-gather.23.cloned.1.call-start = ((), (), s32[]{:S(2)}) async-start(), calls=%async_computation.11 | async-start | bytes 8257536 | tf_op jit(solution)/shard_map/all_gather | solution.py:183
  267.3 284.9 %reduce-scatter.5.cloned.1.call-start = ((), (), s32[]{:S(2)}) async-start(), calls=%async_computation.12 | async-start | bytes 4456448 | tf_op jit(solution)/shard_map/reduce_scatter | solution.py:184
  474.6 0.7 copy-start.17
  474.6 1.0 copy-start.4
  474.6 1.0 copy-start.6
  476.0 76.3 %copy-start.2 = (bf16[32,4096]{1,0:T(8,128)(2,1)S(1)}, bf16[32,4096]{1,0:T(8,128)(2,1)}, u32[]{:S(2)}) copy-start(bf16[32,4096]{1,0:T(8,128)(2,1)} %reduce-scatter.3.cloned.1.call-done) | copy-start | bytes 786436
  477.7 9.4 %all-to-all-start = ((bf16[8,2,4096]{2,1,0:T(2,128)(2,1)}), bf16[8,2,4096]{2,1,0:T(2,128)(2,1)S(1)}, u32[]{:S(2)}, u32[]{:S(2)}) async-start(bf16[8,2,4096]{2,1,0:T(2,128)(2,1)} %reshape.472), calls=%async_computation.2 | async-start | bytes 262144 | tf_op jit(solution)/shard_map/all_to_all | solution.py:224
Sparse Core Ops, SparseCore 0:
  11.0 53.8 all-gather.8
  66.6 25.9 all-gather.10
  94.2 24.0 all-gather.12
  119.9 25.1 all-gather.14
  188.8 74.0 reduce-scatter.2
  264.5 44.9 all-gather.18
  312.5 51.3 all-gather.16
  365.7 45.2 all-gather.20
  412.8 45.4 all-gather.22
  474.7 77.5 reduce-scatter.4
